TPU v7x, 32 devices: a whole 2x2x4 slice. The times are simulated.
32 devices in a mesh: dp: 8 (over y, x, core), tensor: 4 (over z).
Axes of the slice: x: 2, y: 2, z: 4, core: 2. Of those that a mesh axis runs over, the one named last changes fastest.
Arguments:
- tokens: bfloat16 [4096, 2048], P('dp'), may hold values from -6 to 6
- seq_ids: int32 [4096], replicated, may hold values from 0 to 3, never falling along the last dimension, each value on 1 to 2048 neighbouring positions
- route_ids: int32 [4096, 6], P('dp'), may hold values from 0 to 63, all different within a row; in each aligned block of 512 rows (0 to 511, 512 to 1023, ...) at most 72 rows name the same one
- cotangent: bfloat16 [4096, 2048], P('dp'), may hold values from -6 to 6
- input_gain: float32 [2048], replicated, may hold values from 0.5 to 1.5
- w_query: bfloat16 [2048, 3072], P(None, 'tensor'), may hold values from -0.125 to 0.125
- w_latent: bfloat16 [2048, 576], replicated, may hold values from -0.125 to 0.125
- latent_gain: float32 [512], replicated, may hold values from 0.5 to 1.5
- w_expand: bfloat16 [512, 4096], P(None, 'tensor'), may hold values from -0.25 to 0.25
- w_out: bfloat16 [2048, 2048], P('tensor'), may hold values from -0.5 to 0.5
- middle_gain: float32 [2048], replicated, may hold values from 0.5 to 1.5
- w_router: bfloat16 [2048, 64], replicated, may hold values from -0.0390625 to 0.0390625
- expert_gate: bfloat16 [64, 2048, 1408], P('dp', None, 'tensor'), may hold values from -0.125 to 0.125
- expert_up: bfloat16 [64, 2048, 1408], P('dp', None, 'tensor'), may hold values from -0.125 to 0.125
- expert_down: bfloat16 [64, 1408, 2048], P('dp', 'tensor'), may hold values from -2.5 to 2.5
- shared_gate: bfloat16 [2048, 2816], P(None, 'tensor'), may hold values from -0.125 to 0.125
- shared_up: bfloat16 [2048, 2816], P(None, 'tensor'), may hold values from -0.125 to 0.125
- shared_down: bfloat16 [2816, 2048], P('tensor'), may hold values from -0.21875 to 0.21875
Outputs:
- output: bfloat16 [4096, 2048], P('dp')
- token_grad: bfloat16 [4096, 2048], P('dp')
- grad_input_gain: float32 [2048], P('dp')
- grad_query: float32 [2048, 3072], P('dp', 'tensor')
- grad_latent: float32 [2048, 576], P('dp')
- grad_latent_gain: float32 [512], P('dp')
- grad_expand: float32 [512, 4096], P('dp', 'tensor')
- grad_out_proj: float32 [2048, 2048], P('tensor', 'dp')
- grad_middle_gain: float32 [2048], P('dp')
- grad_router: float32 [2048, 64], P('dp')
- grad_expert_gate: float32 [64, 2048, 1408], P('dp', None, 'tensor')
- grad_expert_up: float32 [64, 2048, 1408], P('dp', None, 'tensor')
- grad_expert_down: float32 [64, 1408, 2048], P('dp', 'tensor')
- grad_shared_gate: float32 [2048, 2816], P('dp', 'tensor')
- grad_shared_up: float32 [2048, 2816], P('dp', 'tensor')
- grad_shared_down: float32 [2816, 2048], P('tensor', 'dp')
Inputs may be any that keep to these rules, and one draw needn't show every extreme that they name: seq_ids never fall; each sequence has 1 to 2048 tokens, one has exactly 2048. `route_ids`: each row names 6 different experts; in the rows of one data block (512 tokens) no expert is named by more than 72 rows, a bound that some block reaches.
All inputs are finite; a program needn't handle non-finite values.
Results may differ from a plain program's by a relative error of at most 0.025.
Values may be sent and summed in bfloat16 or wider, within the bound.
No kernel may reach another device: no remote copies, remote signals or barrier semaphores. Data moves between devices by JAX's collectives and lax.ppermute only.
A program may use at most 448 MiB of HBM per device.

v0:
```python
import jax
import jax.numpy as jnp
from jax import lax
from jax.sharding import PartitionSpec as P

DN = 128
DR = 64
DV = 128
KVR = 512
REACH = 4
CAP = 72
BF = jnp.bfloat16
F32 = jnp.float32
epsilon = 1e-06


def dot(eq, a, b):
    return jnp.einsum(eq, a, b, preferred_element_type=F32)


def passed_along(shard, axis, by):
    peers = lax.axis_size(axis)
    pairs = [(i, i + by) for i in range(peers) if 0 <= i + by < peers]
    return lax.ppermute(shard, axis, pairs)


def normed(values, norm_gain):
    return (
        values * lax.rsqrt(jnp.mean(values * values, axis=-1, keepdims=True) + epsilon) * norm_gain
    )


def norm_backward(values, norm_gain, upstream):
    _, pullback = jax.vjp(normed, values, norm_gain)
    return pullback(upstream)


def rotate(values, cosine, sine):
    half = values.shape[-1] // 2
    front, back = (values[..., :half], values[..., half:])
    return jnp.concatenate([front * cosine - back * sine, back * cosine + front * sine], axis=-1)


def rotate_back(upstream, cosine, sine):
    return rotate(upstream, cosine, -sine)


def silu_gate(gate_val, up_val):
    return gate_val * jax.nn.sigmoid(gate_val) * up_val


def silu_backward(gate_val, up_val, upstream):
    _, pullback = jax.vjp(silu_gate, gate_val, up_val)
    return pullback(upstream)


def rope_tables(seq_all, seq_here, index_here):
    starts = jnp.sum((seq_all[None, :] < seq_here[:, None]).astype(jnp.int32), axis=1)
    position = (index_here - starts).astype(F32)
    frequency = 10000.0 ** (-(jnp.arange(DR // 2, dtype=F32) * 2.0) / DR)
    angle = position[:, None] * frequency[None, :]
    return (jnp.cos(angle), jnp.sin(angle))


def scatter_sum(parts):
    joined = jnp.concatenate(parts, axis=1)
    summed = lax.psum_scatter(joined, "dp", scatter_dimension=0, tiled=True)
    out, at = ([], 0)
    for part in parts:
        out.append(summed[:, at : at + part.shape[1]].astype(F32))
        at += part.shape[1]
    return out


def shards(
    tokens,
    seq_ids,
    route_ids,
    cotangent,
    input_gain,
    w_query,
    w_latent,
    latent_gain,
    w_expand,
    w_out,
    middle_gain,
    w_router,
    expert_gate,
    expert_up,
    expert_down,
    shared_gate,
    shared_up,
    shared_down,
):
    devices = lax.axis_size("dp")
    rank_dp = lax.axis_index("dp")
    tok_rows, width = tokens.shape
    experts_local = expert_gate.shape[0]
    heads_local = w_query.shape[1] // (DN + DR)
    reach = min(REACH, devices - 1)
    window = (reach + 1) * tok_rows
    scale = (DN + DR) ** (-0.5)
    cot_all = lax.all_gather(cotangent, "dp", tiled=True)
    route_all = lax.all_gather(route_ids, "dp", tiled=True)
    index_here = rank_dp * tok_rows + jnp.arange(tok_rows, dtype=jnp.int32)
    seq_here = lax.dynamic_slice_in_dim(seq_ids, rank_dp * tok_rows, tok_rows, 0)
    cosine, sine = rope_tables(seq_ids, seq_here, index_here)
    key_index = (rank_dp - reach) * tok_rows + jnp.arange(window, dtype=jnp.int32)
    seq_padded = jnp.concatenate([jnp.full((reach * tok_rows,), -1, jnp.int32), seq_ids])
    seq_keys = lax.dynamic_slice_in_dim(seq_padded, rank_dp * tok_rows, window, 0)
    allowed = (seq_here[:, None] == seq_keys[None, :]) & (key_index[None, :] <= index_here[:, None])
    token_features = tokens.astype(F32)
    grad_output = cotangent.astype(F32)
    hidden_in = normed(token_features, input_gain).astype(BF)
    latent_full = jnp.dot(hidden_in, w_latent, preferred_element_type=F32)
    latent_raw = latent_full[:, :KVR]
    latent = normed(latent_raw, latent_gain).astype(BF)
    rope_key = rotate(latent_full[:, KVR:], cosine, sine).astype(BF)
    own_keys = jnp.concatenate([latent, rope_key], axis=1)
    earlier = [passed_along(own_keys, "dp", back) for back in range(reach, 0, -1)]
    keys_window = jnp.concatenate(earlier + [own_keys], axis=0)
    latent_window = keys_window[:, :KVR]
    rope_window = keys_window[:, KVR:]
    query_pre = jnp.dot(hidden_in, w_query, preferred_element_type=F32).reshape(
        tok_rows, heads_local, DN + DR
    )
    queries = jnp.concatenate(
        [query_pre[..., :DN], rotate(query_pre[..., DN:], cosine[:, None, :], sine[:, None, :])],
        axis=-1,
    ).astype(BF)
    expanded = (
        jnp.dot(latent_window, w_expand, preferred_element_type=F32)
        .astype(BF)
        .reshape(window, heads_local, DN + DV)
    )
    key_nope = expanded[..., :DN]
    key_value = expanded[..., DN:]
    scores = dot("qhd,khd->hqk", queries[..., :DN], key_nope) + dot(
        "qhd,kd->hqk", queries[..., DN:], rope_window
    )
    scores = jnp.where(allowed[None], scores * scale, -1e30)
    probs = jax.nn.softmax(scores, axis=-1)
    probs_low = probs.astype(BF)
    attended = (
        dot("hqk,khd->qhd", probs_low, key_value).astype(BF).reshape(tok_rows, heads_local * DV)
    )
    attention = lax.psum(
        jnp.dot(attended, w_out, preferred_element_type=F32).astype(BF), "tensor"
    ).astype(F32)
    middle = token_features + attention
    hidden_mid = normed(middle, middle_gain).astype(BF)
    hidden_all = lax.all_gather(hidden_mid, "dp", tiled=True)
    shared_gate_val = jnp.dot(hidden_mid, shared_gate, preferred_element_type=F32)
    shared_up_val = jnp.dot(hidden_mid, shared_up, preferred_element_type=F32)
    shared_active = silu_gate(shared_gate_val, shared_up_val).astype(BF)
    shared_result = jnp.dot(shared_active, shared_down, preferred_element_type=F32)
    shared_active_grad = dot("td,fd->tf", cotangent, shared_down)
    shared_gate_grad, shared_up_grad = silu_backward(
        shared_gate_val, shared_up_val, shared_active_grad
    )
    shared_gate_grad = shared_gate_grad.astype(BF)
    shared_up_grad = shared_up_grad.astype(BF)
    mid_from_shared = dot("tf,df->td", shared_gate_grad, shared_gate) + dot(
        "tf,df->td", shared_up_grad, shared_up
    )
    grad_shared_down = dot("td,tf->df", cotangent, shared_active).astype(BF)
    grad_shared_gate = dot("td,tf->df", hidden_mid, shared_gate_grad).astype(BF)
    grad_shared_up = dot("td,tf->df", hidden_mid, shared_up_grad).astype(BF)
    local_ids = rank_dp * experts_local + jnp.arange(experts_local, dtype=jnp.int32)
    named = jnp.any(route_all[:, :, None] == local_ids[None, None, :], axis=1)
    named_block = named.reshape(devices, tok_rows, experts_local)
    before = jnp.tril(jnp.ones((tok_rows, tok_rows), BF), -1)
    rank_within = dot("ts,bse->bet", before, named_block.astype(BF)).astype(jnp.int32)
    slot = jnp.where(named_block.transpose(0, 2, 1), rank_within, -1)
    chosen = (slot[:, :, None, :] == jnp.arange(CAP, dtype=jnp.int32)[None, None, :, None]).astype(
        BF
    )
    logits = jnp.dot(hidden_all, w_router, preferred_element_type=F32)
    router_probs = jax.nn.softmax(logits, axis=-1)
    local_probs = lax.dynamic_slice_in_dim(
        router_probs, rank_dp * experts_local, experts_local, 1
    ).reshape(devices, tok_rows, experts_local)
    slot_gates = jnp.sum(
        chosen.astype(F32) * local_probs.transpose(0, 2, 1)[:, :, None, :], axis=-1
    )
    cot_rows = dot("bect,btd->becd", chosen, cot_all.reshape(devices, tok_rows, width)).astype(BF)
    rows = dot("bect,btd->becd", chosen, hidden_all.reshape(devices, tok_rows, width)).astype(BF)
    gate_val = dot("becd,edf->becf", rows, expert_gate)
    up_val = dot("becd,edf->becf", rows, expert_up)
    down_back = dot("becd,efd->becf", cot_rows, expert_down)
    active = silu_gate(gate_val, up_val).astype(BF)
    gated_active = active.astype(F32) * slot_gates[..., None]
    gate_grad = jnp.sum(active.astype(F32) * down_back, axis=-1)
    gate_val_grad, up_val_grad = silu_backward(gate_val, up_val, down_back * slot_gates[..., None])
    gate_val_grad = gate_val_grad.astype(BF)
    up_val_grad = up_val_grad.astype(BF)
    gated_active = gated_active.astype(BF)
    row_grad = (
        dot("becf,edf->becd", gate_val_grad, expert_gate)
        + dot("becf,edf->becd", up_val_grad, expert_up)
    ).astype(BF)
    row_out = dot("becf,efd->becd", gated_active, expert_down).astype(BF)
    probs_grad = dot("bect,bec->bte", chosen, gate_grad.astype(BF)).reshape(-1, experts_local)
    probs_grad = lax.dynamic_update_slice_in_dim(
        jnp.zeros_like(router_probs), probs_grad, rank_dp * experts_local, 1
    )
    logit_grad = (
        router_probs * (probs_grad - jnp.sum(router_probs * probs_grad, axis=-1, keepdims=True))
    ).astype(BF)
    grad_router = dot("td,te->de", hidden_all, logit_grad)
    mid_part = dot("bect,becd->btd", chosen, row_grad).reshape(-1, width) + dot(
        "te,de->td", logit_grad, w_router
    )
    mid_block = lax.psum_scatter(mid_part.astype(BF), "dp", scatter_dimension=0, tiled=True)
    mid_grad = lax.psum((mid_block.astype(F32) + mid_from_shared).astype(BF), "tensor").astype(F32)
    routed_part = dot("bect,becd->btd", chosen, row_out).reshape(-1, width).astype(BF)
    routed_part, _ = lax.optimization_barrier((routed_part, mid_block))
    routed_block = lax.psum_scatter(routed_part, "dp", scatter_dimension=0, tiled=True)
    grad_expert_down = dot("becf,becd->efd", gated_active, cot_rows)
    grad_expert_gate = dot("becd,becf->edf", rows, gate_val_grad)
    grad_expert_up = dot("becd,becf->edf", rows, up_val_grad)
    middle_from_norm, grad_middle_gain = norm_backward(middle, middle_gain, mid_grad)
    middle_grad = grad_output + middle_from_norm
    middle_low = middle_grad.astype(BF)
    grad_out_proj = dot("td,tc->dc", middle_low, attended).astype(BF)
    attended_grad = (
        dot("td,cd->tc", middle_low, w_out).astype(BF).reshape(tok_rows, heads_local, DV)
    )
    probs_grad_att = dot("qhd,khd->hqk", attended_grad, key_value)
    score_grad = (
        probs * (probs_grad_att - jnp.sum(probs * probs_grad_att, axis=-1, keepdims=True))
    ).astype(BF)
    query_nope_grad = dot("hqk,khd->qhd", score_grad, key_nope) * scale
    query_rope_grad = dot("hqk,kd->qhd", score_grad, rope_window) * scale
    key_nope_grad = dot("hqk,qhd->khd", score_grad, queries[..., :DN]) * scale
    rope_window_grad = dot("hqk,qhd->kd", score_grad, queries[..., DN:]) * scale
    value_grad = dot("hqk,qhd->khd", probs_low, attended_grad)
    expanded_grad = (
        jnp.concatenate([key_nope_grad, value_grad], axis=-1)
        .astype(BF)
        .reshape(window, heads_local * (DN + DV))
    )
    latent_window_grad = dot("wc,kc->wk", expanded_grad, w_expand)
    grad_expand = dot("wk,wc->kc", latent_window, expanded_grad).astype(BF)
    window_grad = jnp.concatenate([latent_window_grad, rope_window_grad], axis=1)
    keys_grad = window_grad[reach * tok_rows :]
    for back in range(reach, 0, -1):
        start = (reach - back) * tok_rows
        piece = window_grad[start : start + tok_rows].astype(BF)
        keys_grad = keys_grad + passed_along(piece, "dp", -back).astype(F32)
    query_grad = (
        jnp.concatenate(
            [query_nope_grad, rotate_back(query_rope_grad, cosine[:, None, :], sine[:, None, :])],
            axis=-1,
        )
        .astype(BF)
        .reshape(tok_rows, heads_local * (DN + DR))
    )
    grad_query = dot("td,tc->dc", hidden_in, query_grad).astype(BF)
    input_from_query = dot("tc,dc->td", query_grad, w_query)
    keys_grad = lax.psum(keys_grad.astype(BF), "tensor").astype(F32)
    latent_raw_grad, grad_latent_gain = norm_backward(latent_raw, latent_gain, keys_grad[:, :KVR])
    rope_raw_grad = rotate_back(keys_grad[:, KVR:], cosine, sine)
    latent_full_grad = jnp.concatenate([latent_raw_grad, rope_raw_grad], axis=-1).astype(BF)
    grad_latent = dot("td,tc->dc", hidden_in, latent_full_grad).astype(BF)
    input_grad = lax.psum(input_from_query.astype(BF), "tensor").astype(F32) + dot(
        "tc,dc->td", latent_full_grad, w_latent
    )
    token_from_norm, grad_input_gain = norm_backward(token_features, input_gain, input_grad)
    token_grad = (middle_grad + token_from_norm).astype(BF)
    routed_block, _ = lax.optimization_barrier((routed_block, mid_grad))
    feedforward = lax.psum((routed_block.astype(F32) + shared_result).astype(BF), "tensor")
    output = (middle + feedforward.astype(F32)).astype(BF)
    grad_shared_down, grad_shared_gate, grad_shared_up = scatter_sum(
        [grad_shared_down, grad_shared_gate, grad_shared_up]
    )
    grad_router = lax.psum(grad_router.astype(BF), "tensor")
    gains = jnp.stack(
        [grad_middle_gain, grad_input_gain, jnp.repeat(grad_latent_gain, width // KVR)], axis=1
    ).astype(BF)
    grad_out_proj, grad_query, grad_latent, grad_expand, grad_router, gains = scatter_sum(
        [grad_out_proj, grad_query, grad_latent, grad_expand.reshape(width, -1), grad_router, gains]
    )
    grad_expand = grad_expand.reshape(KVR // devices, -1)
    return (
        output,
        token_grad,
        gains[:, 1],
        grad_query,
        grad_latent,
        gains[:: width // KVR, 2],
        grad_expand,
        grad_out_proj.T,
        gains[:, 0],
        grad_router,
        grad_expert_gate,
        grad_expert_up,
        grad_expert_down,
        grad_shared_gate,
        grad_shared_up,
        grad_shared_down.T,
    )


def solution(mesh):
    placed = (
        P("dp", None),
        P(),
        P("dp", None),
        P("dp", None),
        P(),
        P(None, "tensor"),
        P(),
        P(),
        P(None, "tensor"),
        P("tensor", None),
        P(),
        P(),
        P("dp", None, "tensor"),
        P("dp", None, "tensor"),
        P("dp", "tensor", None),
        P(None, "tensor"),
        P(None, "tensor"),
        P("tensor", None),
    )
    return jax.shard_map(
        shards,
        mesh=mesh,
        in_specs=placed,
        out_specs=(
            P("dp", None),
            P("dp", None),
            P("dp"),
            P("dp", "tensor"),
            P("dp", None),
            P("dp"),
            P("dp", "tensor"),
            P("tensor", "dp"),
            P("dp"),
            P("dp", None),
            P("dp", None, "tensor"),
            P("dp", None, "tensor"),
            P("dp", "tensor", None),
            P("dp", "tensor"),
            P("dp", "tensor"),
            P("tensor", "dp"),
        ),
        check_vma=False,
    )
```

profile of v0, /device:TPU:0, one launch (start us, length us, event | category | flops | bytes accessed | tf_op | source)
XLA Modules:
  0.0 1195.1 jit_solution(14079437632044810351)
XLA Ops:
  40.0 25.1 %collective-permute-done = bf16[512,576]{0,1:T(8,128)(2,1)} collective-permute-done((bf16[512,576]{0,1:T(8,128)(2,1)}, bf16[512,576]{0,1:T(8,128)(2,1)}, u32[]{:S(2)}, u32[]{:S(2)}) %collective-permute-start) | collective-permute-done | bytes 589856 | tf_op jit(solution)/shard_map/ppermute | solution.py:24
  73.0 8.9 fusion.82
  82.0 13.6 %fusion.3 = f32[4,512,2560]{2,1,0:T(8,128)} fusion(f32[4,512,2560]{2,1,0:T(8,128)} %fusion.82, pred[512,2560]{1,0:T(8,128)(4,1)S(1)} %compare_and_fusion, bf16[2560,576]{0,1:T(8,128)(2,1)} %copy-done.37, bf16[512,4,32]{0,2,1:T(8,128)(2,1)S(1)} %get-tuple-element.126, bf16[512,4,32]{0,2,1:T(8,128)(2,1)S(1)} %get-tuple-element.125), kind=kOutput, calls=%fused_computation.7 | convolution fusion | flops 687341568 | bytes 43843584 | tf_op jit(solution)/shard_map/qhd,kd->hqk/dot_general | solution.py:18
  95.6 23.5 %fusion.169 = (f32[4,512]{1,0:T(4,128)S(1)}, f32[4,512,2560]{2,1,0:T(8,128)}) fusion(f32[4,512,2560]{2,1,0:T(8,128)} %fusion.3), kind=kOutput, calls=%fused_computation.251 | output fusion | flops 10488319 | bytes 41951232 | tf_op jit(solution)/shard_map/sub | solution.py:142
  119.1 17.4 %fusion.105 = bf16[4,128,512]{2,1,0:T(8,128)(2,1)} fusion(bf16[2560,4,256]{0,2,1:T(8,128)(2,1)} %bitcast.238, f32[4,512]{1,0:T(4,128)S(1)} %get-tuple-element.144, f32[4,512,2560]{2,1,0:T(8,128)} %fusion.3), kind=kOutput, calls=%fused_computation.147 | convolution fusion | flops 1358172672 | bytes 45096960 | tf_op jit(solution)/shard_map/hqk,khd->qhd/dot_general | solution.py:18
  141.5 91.4 %all-reduce.6.cloned.1.call-done = bf16[512,2048]{1,0:T(8,128)(2,1)} async-done(((bf16[512,2048]{1,0:T(8,128)(2,1)}), bf16[512,2048]{1,0:T(8,128)(2,1)}) %all-reduce.6.cloned.1.call-update) | async-done | bytes 2097168 | tf_op jit(solution)/shard_map/psum | solution.py:147
  239.6 9.4 all_gather.9
  252.7 18.8 %convolution_convert_fusion = bf16[8,8,72,2048]{3,2,1,0:T(8,128)(2,1)} fusion(bf16[8,512,2048,1]{2,1,3,0:T(8,128)(2,1)} %bitcast.249, s32[8,8,512]{2,1,0:T(8,128)S(1)} %fusion.120), kind=kOutput, calls=%fused_computation.26 | convolution fusion | flops 9675472896 | bytes 35782656 | tf_op jit(solution)/shard_map/bect,btd->becd/dot_general | solution.py:18
  271.4 59.2 %all-gather.3.cloned.1.call-done = bf16[4096,2048]{1,0:T(8,128)(2,1)} async-done(((bf16[512,2048]{1,0:T(8,128)(2,1)}), bf16[4096,2048]{1,0:T(8,128)(2,1)}) %all-gather.3.cloned.1.call-update) | async-done | bytes 16777232 | tf_op jit(solution)/shard_map/all_gather | solution.py:152
  330.6 18.8 %convolution_convert_fusion.1 = bf16[8,8,72,2048]{3,2,1,0:T(8,128)(2,1)} fusion(bf16[8,512,2048,1]{2,1,3,0:T(8,128)(2,1)} %bitcast.222, s32[8,8,512]{2,1,0:T(8,128)S(1)} %fusion.120), kind=kOutput, calls=%fused_computation.27 | convolution fusion | flops 9675472896 | bytes 35782656 | tf_op jit(solution)/shard_map/bect,btd->becd/dot_general | solution.py:18
  349.4 20.0 %fusion.18 = f32[8,8,72,352]{3,2,1,0:T(8,128)} fusion(bf16[8,8,72,2048]{3,2,1,0:T(8,128)(2,1)} %convolution_convert_fusion.1, bf16[8,2048,352]{1,2,0:T(8,128)(2,1)} %param.31), kind=kOutput, calls=%fused_computation.22 | convolution fusion | flops 6643777536 | bytes 36896768 | tf_op jit(solution)/shard_map/becd,edf->becf/dot_general | solution.py:18
  369.4 20.4 %fusion.20 = f32[8,8,72,352]{3,2,1,0:T(8,128)} fusion(bf16[8,8,72,2048]{3,2,1,0:T(8,128)(2,1)} %convolution_convert_fusion.1, bf16[8,2048,352]{1,2,0:T(8,128)(2,1)} %param.30), kind=kOutput, calls=%fused_computation.24 | convolution fusion | flops 6643777536 | bytes 36896768 | tf_op jit(solution)/shard_map/becd,edf->becf/dot_general | solution.py:18
  389.9 24.2 %fusion.39 = (bf16[8,8,72]{2,0,1:T(8,128)(2,1)S(1)}, bf16[8,8,72,352]{3,2,0,1:T(8,128)(2,1)}, f32[8,8,72,352]{3,2,1,0:T(8,128)}) fusion(f32[8,8,72,352]{3,2,1,0:T(8,128)} %fusion.18, f32[8,8,72,352]{3,2,1,0:T(8,128)} %fusion.20, bf16[8,352,2048]{2,1,0:T(8,128)(2,1)} %param.32, bf16[8,8,72,2048]{3,2,1,0:T(8,128)(2,1)} %convolution_convert_fusion), kind=kOutput, calls=%fused_computation.56 | convolution fusion | flops 6658371072 | bytes 53126144 | tf_op jit(solution)/shard_map/becd,efd->becf/dot_general | solution.py:18
  415.7 11.1 fusion.170
  436.6 21.0 %fusion.31 = f32[8,8,72,2048]{3,2,0,1:T(8,128)} fusion(bf16[8,2048,352]{1,2,0:T(8,128)(2,1)} %param.30, bf16[8,8,72,352]{3,2,0,1:T(8,128)(2,1)} %get-tuple-element.115), kind=kOutput, calls=%fused_computation.33 | convolution fusion | flops 6643777536 | bytes 52527104 | tf_op jit(solution)/shard_map/becf,edf->becd/dot_general | solution.py:18
  457.6 40.2 %fusion.5 = f32[8,512,2048,1]{2,1,3,0:T(8,128)} fusion(f32[8,8,72,2048]{3,2,0,1:T(8,128)} %fusion.31, bf16[8,2048,352]{1,2,0:T(8,128)(2,1)} %param.31, bf16[8,8,72,352]{3,2,0,1:T(8,128)(2,1)} %get-tuple-element.114, pred[8,8,72,512]{3,2,1,0:T(8,128)(4,1)} %iota_compare_fusion.14), kind=kOutput, calls=%fused_computation.12 | convolution fusion | flops 16326328320 | bytes 88440832 | tf_op jit(solution)/shard_map/bect,becd->btd/dot_general | solution.py:18
  497.8 17.1 %fusion.1 = bf16[4096,2048]{1,0:T(8,128)(2,1)} fusion(f32[8,512,2048,1]{2,1,3,0:T(8,128)} %fusion.5, bf16[4096,64]{0,1:T(8,128)(2,1)} %multiply_convert_fusion.6, bf16[2048,64]{0,1:T(8,128)(2,1)S(1)} %copy-done.31), kind=kOutput, calls=%fused_computation.3 | convolution fusion | flops 1090519040 | bytes 51118080 | tf_op jit(solution)/shard_map/te,de->td/dot_general | solution.py:18
  534.9 95.9 %reduce-scatter.5.cloned.1.call-done = bf16[512,2048]{1,0:T(8,128)(2,1)} async-done(((bf16[4096,2048]{1,0:T(8,128)(2,1)}), bf16[512,2048]{1,0:T(8,128)(2,1)}) %reduce-scatter.5.cloned.1.call-update) | async-done | bytes 2097168 | tf_op jit(solution)/shard_map/reduce_scatter | solution.py:214
  630.9 7.1 add_convert_fusion.3
  638.2 29.4 %bitcast_convert_fusion = bf16[8,512,2048]{2,1,0:T(8,128)(2,1)} fusion(bf16[8,352,2048]{2,1,0:T(8,128)(2,1)} %param.32, bf16[8,8,72,352]{3,2,0,1:T(8,128)(2,1)} %get-tuple-element.136, pred[8,8,72,512]{3,2,1,0:T(8,128)(4,1)} %iota_compare_fusion.13), kind=kOutput, calls=%fused_computation.4 | convolution fusion | flops 16325279744 | bytes 33914880 | tf_op jit(solution)/shard_map/bect,becd->btd/dot_general | solution.py:18
  667.7 10.2 convolution_convert_fusion.11
  677.9 46.8 %all-reduce.8.cloned.1.call-done = bf16[512,2048]{1,0:T(8,128)(2,1)} async-done(((bf16[512,2048]{1,0:T(8,128)(2,1)}), bf16[512,2048]{1,0:T(8,128)(2,1)}) %all-reduce.8.cloned.1.call-update) | async-done | bytes 2097168 | tf_op jit(solution)/shard_map/psum | solution.py:215
  735.0 19.7 %fusion.69 = bf16[2560,4,128]{0,2,1:T(8,128)(2,1)} fusion(bf16[512,4,128]{0,2,1:T(8,128)(2,1)} %bitcast.252, f32[4,512]{1,0:T(4,128)S(1)} %copy-done.48, f32[4,512,2560]{2,1,0:T(8,128)} %fusion.3), kind=kOutput, calls=%fused_computation.106 | convolution fusion | flops 1359221248 | bytes 24125440 | tf_op jit(solution)/shard_map/hqk,qhd->khd/dot_general | solution.py:18
  754.7 15.2 %multiply_reduce_fusion = (f32[4,512]{1,0:T(4,128)S(1)}, f32[4,512,2560]{2,1,0:T(8,128)}) fusion(f32[4,512,2560]{2,1,0:T(8,128)} %get-tuple-element.145, f32[4,512]{1,0:T(4,128)S(1)} %copy-done.48, bf16[512,4,128]{0,2,1:T(8,128)(2,1)} %bitcast.253, bf16[2560,4,256]{0,2,1:T(8,128)(2,1)} %bitcast.239), kind=kOutput, calls=%fused_computation.9 | convolution fusion | flops 1357903872 | bytes 45105152 | tf_op jit(solution)/shard_map/qhd,khd->hqk/dot_general | solution.py:18
  769.9 14.6 %multiply_convert_fusion = bf16[4,512,2560]{2,1,0:T(8,128)(2,1)S(1)} fusion(f32[4,512,2560]{2,1,0:T(8,128)} %get-tuple-element.150, f32[4,512]{1,0:T(4,128)S(1)} %get-tuple-element.149, f32[4,512,2560]{2,1,0:T(8,128)} %get-tuple-element.145, f32[4,512]{1,0:T(4,128)S(1)} %copy-done.48), kind=kLoop, calls=%fused_computation.8 | loop fusion | flops 20971520 | bytes 52445184 | tf_op jit(solution)/shard_map/convert_element_type | solution.py:232
  843.4 7.2 fusion.92
  864.7 178.7 %all-reduce.10.cloned.1.call-done = (bf16[512,2048]{1,0:T(8,128)(2,1)}, bf16[512,2048]{1,0:T(8,128)(2,1)}, bf16[512,576]{0,1:T(8,128)(2,1)}, bf16[2048,64]{0,1:T(8,128)(2,1)}) async-done(((bf16[512,2048]{1,0:T(8,128)(2,1)}, bf16[512,2048]{1,0:T(8,128)(2,1)}, bf16[512,576]{0,1:T(8,128)(2,1)}, bf16[2048,64]{0,1:T(8,128)(2,1)}), (bf16[512,2048]{1,0:T(8,128)(2,1)}, bf16[512,2048]{1,0:T(8,128)(2,1)}, ...) | async-done | bytes 5046288 | tf_op jit(solution)/shard_map/psum | solution.py:272
  1059.2 40.1 %concatenate.47 = bf16[2048,2179]{0,1:T(8,128)(2,1)} concatenate(bf16[2048,512]{0,1:T(8,128)(2,1)} %convolution_convert_fusion.8, bf16[2048,768]{0,1:T(8,128)(2,1)} %convolution_convert_fusion.3, bf16[2048,576]{0,1:T(8,128)(2,1)} %convolution_convert_fusion.7, bf16[2048,256]{0,1:T(8,128)(2,1)} %copy.126, bf16[2048,64]{0,1:T(8,128)(2,1)S(1)} %copy-done.39, ...), dimensions={1} | concatenate | bytes 17850368 | tf_op jit(solution)/shard_map/concatenate | solution.py:66
  1101.9 21.4 %convolution_bitcast_fusion = f32[8,2048,352]{1,2,0:T(8,128)} fusion(bf16[8,8,72,2048]{3,2,1,0:T(8,128)(2,1)} %convolution_convert_fusion.1, bf16[8,8,72,352]{3,2,0,1:T(8,128)(2,1)} %get-tuple-element.114), kind=kOutput, calls=%fused_computation.53 | convolution fusion | flops 6643777536 | bytes 45187072 | tf_op jit(solution)/shard_map/becd,becf->edf/dot_general | solution.py:18
  1123.3 22.3 %convolution_bitcast_fusion.1 = f32[8,2048,352]{1,2,0:T(8,128)} fusion(bf16[8,8,72,2048]{3,2,1,0:T(8,128)(2,1)} %convolution_convert_fusion.1, bf16[8,8,72,352]{3,2,0,1:T(8,128)(2,1)S(1)} %copy-done.8), kind=kOutput, calls=%fused_computation.54 | convolution fusion | flops 6643777536 | bytes 45187072 | tf_op jit(solution)/shard_map/becd,becf->edf/dot_general | solution.py:18
  1145.6 18.2 %fusion.35 = f32[8,352,2048]{2,1,0:T(8,128)} fusion(bf16[8,8,72,352]{3,2,0,1:T(8,128)(2,1)} %get-tuple-element.136, bf16[8,8,72,2048]{3,2,1,0:T(8,128)(2,1)} %convolution_convert_fusion), kind=kOutput, calls=%fused_computation.52 | convolution fusion | flops 6643777536 | bytes 45187072 | tf_op jit(solution)/shard_map/becf,becd->efd/dot_general | solution.py:18
  1163.7 8.7 fusion.66
  (299 shorter events, 202.8 us)
Async XLA Ops:
  8.0 28.3 %copy-start = (bf16[2048,768]{1,0:T(8,128)(2,1)S(1)}, bf16[2048,768]{1,0:T(8,128)(2,1)}, u32[]{:S(2)}) copy-start(bf16[2048,768]{1,0:T(8,128)(2,1)} %param.23) | copy-start | bytes 9437188
  8.0 224.8 %all-reduce.6.cloned.1.call-start = ((), (), s32[]{:S(2)}) async-start(), calls=%async_computation.4 | async-start | bytes 4194304 | tf_op jit(solution)/shard_map/psum | solution.py:147
  20.9 44.2 %collective-permute-start = (bf16[512,576]{0,1:T(8,128)(2,1)}, bf16[512,576]{0,1:T(8,128)(2,1)}, u32[]{:S(2)}, u32[]{:S(2)}) collective-permute-start(bf16[512,576]{0,1:T(8,128)(2,1)} %pad_maximum_fusion.4), channel_id=1, source_target_pairs={{0,16},{4,20},{8,24},{12,28},{1,17},{5,21},{9,25},{13,29},{2,18},{... | collective-permute-start | bytes 1769480 | tf_op jit(solution)/shard_map/ppermute | solution.py:24
  26.6 39.6 %collective-permute-start.1 = (bf16[512,576]{0,1:T(8,128)(2,1)}, bf16[512,576]{0,1:T(8,128)(2,1)}, u32[]{:S(2)}, u32[]{:S(2)}) collective-permute-start(bf16[512,576]{0,1:T(8,128)(2,1)} %pad_maximum_fusion.4), channel_id=1, source_target_pairs={{0,12},{4,16},{8,20},{12,24},{16,28},{1,13},{5,17},{9,21},{13,25},... | collective-permute-start | bytes 1769480 | tf_op jit(solution)/shard_map/ppermute | solution.py:24
  29.9 37.3 %collective-permute-start.2 = (bf16[512,576]{0,1:T(8,128)(2,1)}, bf16[512,576]{0,1:T(8,128)(2,1)}, u32[]{:S(2)}, u32[]{:S(2)}) collective-permute-start(bf16[512,576]{0,1:T(8,128)(2,1)} %pad_maximum_fusion.4), channel_id=1, source_target_pairs={{0,8},{4,12},{8,16},{12,20},{16,24},{20,28},{1,9},{5,13},{9,17},{1... | collective-permute-start | bytes 1769480 | tf_op jit(solution)/shard_map/ppermute | solution.py:24
  32.9 35.5 %collective-permute-start.3 = (bf16[512,576]{0,1:T(8,128)(2,1)}, bf16[512,576]{0,1:T(8,128)(2,1)}, u32[]{:S(2)}, u32[]{:S(2)}) collective-permute-start(bf16[512,576]{0,1:T(8,128)(2,1)} %pad_maximum_fusion.4), channel_id=1, source_target_pairs={{0,4},{4,8},{8,12},{12,16},{16,20},{20,24},{24,28},{1,5},{5,9},{9,... | collective-permute-start | bytes 1769480 | tf_op jit(solution)/shard_map/ppermute | solution.py:24
  39.8 33.2 %copy-start.22 = (f32[512,768]{0,1:T(8,128)}, f32[512,768]{0,1:T(8,128)S(1)}, u32[]{:S(2)}) copy-start(f32[512,768]{0,1:T(8,128)S(1)} %fusion.159) | copy-start | bytes 4718596
  39.8 29.7 %copy-start.21 = (bf16[512,512]{0,1:T(8,128)(2,1)S(1)}, bf16[512,512]{0,1:T(8,128)(2,1)}, u32[]{:S(2)}) copy-start(bf16[512,512]{0,1:T(8,128)(2,1)} %copy-done.20) | copy-start | bytes 1572868
  39.8 29.7 %copy-start.69 = (bf16[512,1024]{1,0:T(8,128)(2,1)S(1)}, bf16[512,1024]{1,0:T(8,128)(2,1)}, u32[]{:S(2)}) copy-start(bf16[512,1024]{1,0:T(8,128)(2,1)} %param.26) | copy-start | bytes 3145732
  39.9 42.0 %copy-start.27 = (bf16[512,4,32]{0,2,1:T(8,128)(2,1)}, bf16[512,4,32]{0,2,1:T(8,128)(2,1)S(1)}, u32[]{:S(2)}) copy-start(bf16[512,4,32]{0,2,1:T(8,128)(2,1)S(1)} %get-tuple-element.125) | copy-start | bytes 393220
  40.0 42.0 %copy-start.29 = (bf16[512,4,32]{0,2,1:T(8,128)(2,1)}, bf16[512,4,32]{0,2,1:T(8,128)(2,1)S(1)}, u32[]{:S(2)}) copy-start(bf16[512,4,32]{0,2,1:T(8,128)(2,1)S(1)} %get-tuple-element.126) | copy-start | bytes 393220
  140.8 96.3 %copy-start.41 = (f32[2048]{0:T(1024)S(1)}, f32[2048]{0:T(1024)}, u32[]{:S(2)}) copy-start(f32[2048]{0:T(1024)} %param.28) | copy-start | bytes 24580
  140.9 111.8 %all-gather.5.cloned.1.call-start = ((), (), s32[]{:S(2)}) async-start(), calls=%async_computation.6 | async-start | bytes 18874368 | tf_op jit(solution)/shard_map/all_gather | solution.py:103
  141.4 189.2 %all-gather.3.cloned.1.call-start = ((), (), s32[]{:S(2)}) async-start(), calls=%async_computation.5 | async-start | bytes 18874368 | tf_op jit(solution)/shard_map/all_gather | solution.py:152
  239.6 391.3 %reduce-scatter.5.cloned.1.call-start = ((), (), s32[]{:S(2)}) async-start(), calls=%async_computation.7 | async-start | bytes 18874368 | tf_op jit(solution)/shard_map/reduce_scatter | solution.py:214
  514.9 209.8 %all-reduce.8.cloned.1.call-start = ((), (), s32[]{:S(2)}) async-start(), calls=%async_computation.9 | async-start | bytes 4194304 | tf_op jit(solution)/shard_map/psum | solution.py:215
  638.0 188.3 %reduce-scatter.7.cloned.1.call-start = ((), (), s32[]{:S(2)}) async-start(), calls=%async_computation.8 | async-start | bytes 18874368 | tf_op jit(solution)/shard_map/reduce_scatter | solution.py:218
  667.6 57.1 %copy-start.42 = (f32[2048]{0:T(1024)S(1)}, f32[2048]{0:T(1024)}, u32[]{:S(2)}) copy-start(f32[2048]{0:T(1024)} %param.28) | copy-start | bytes 24580
  667.6 57.1 %copy-start.44 = (f32[512]{0:T(512)S(1)}, f32[512]{0:T(512)}, u32[]{:S(2)}) copy-start(f32[512]{0:T(512)} %copy-done.43) | copy-start | bytes 6148
  667.6 375.7 %all-reduce.10.cloned.1.call-start = ((), (), s32[]{:S(2)}) async-start(), calls=%async_computation.12 | async-start | bytes 10092544 | tf_op jit(solution)/shard_map/psum | solution.py:272
  677.9 51.7 %copy-start.57 = (f32[512]{0:T(512)S(1)}, f32[512]{0:T(512)}, u32[]{:S(2)}) copy-start(f32[512]{0:T(512)} %copy-done.56) | copy-start | bytes 6148
  802.5 21.2 %collective-permute-start.4 = (bf16[512,576]{0,1:T(8,128)(2,1)}, bf16[512,576]{0,1:T(8,128)(2,1)S(1)}, u32[]{:S(2)}, u32[]{:S(2)}) collective-permute-start(bf16[512,576]{0,1:T(8,128)(2,1)} %get-tuple-element.118), channel_id=1, source_target_pairs={{16,0},{20,4},{24,8},{28,12},{17,1},{21,5},{25,9},{29,13},{18,2},{... | collective-permute-start | bytes 1769480 | tf_op jit(solution)/shard_map/ppermute | solution.py:24
  803.8 19.9 %collective-permute-start.5 = (bf16[512,576]{0,1:T(8,128)(2,1)}, bf16[512,576]{0,1:T(8,128)(2,1)S(1)}, u32[]{:S(2)}, u32[]{:S(2)}) collective-permute-start(bf16[512,576]{0,1:T(8,128)(2,1)} %get-tuple-element.121), channel_id=1, source_target_pairs={{12,0},{16,4},{20,8},{24,12},{28,16},{13,1},{17,5},{21,9},{25,13},... | collective-permute-start | bytes 1769480 | tf_op jit(solution)/shard_map/ppermute | solution.py:24
  805.1 18.6 %collective-permute-start.6 = (bf16[512,576]{0,1:T(8,128)(2,1)}, bf16[512,576]{0,1:T(8,128)(2,1)}, u32[]{:S(2)}, u32[]{:S(2)}) collective-permute-start(bf16[512,576]{0,1:T(8,128)(2,1)} %get-tuple-element.120), channel_id=1, source_target_pairs={{8,0},{12,4},{16,8},{20,12},{24,16},{28,20},{9,1},{13,5},{17,9},{2... | collective-permute-start | bytes 1769480 | tf_op jit(solution)/shard_map/ppermute | solution.py:24
  806.4 17.3 %collective-permute-start.7 = (bf16[512,576]{0,1:T(8,128)(2,1)S(1)}, bf16[512,576]{0,1:T(8,128)(2,1)}, u32[]{:S(2)}, u32[]{:S(2)}) collective-permute-start(bf16[512,576]{0,1:T(8,128)(2,1)S(1)} %get-tuple-element.119), channel_id=1, source_target_pairs={{4,0},{8,4},{12,8},{16,12},{20,16},{24,20},{28,24},{5,1},{9,5},{13... | collective-permute-start | bytes 1769480 | tf_op jit(solution)/shard_map/ppermute | solution.py:24
  832.1 267.1 %reduce-scatter.11.cloned.1.call-start = ((), (), s32[]{:S(2)}) async-start(), calls=%async_computation.11 | async-start | bytes 9732096 | tf_op jit(solution)/shard_map/reduce_scatter | solution.py:67
  843.4 329.7 %reduce-scatter.9.cloned.1.call-start = ((), (), s32[]{:S(2)}) async-start(), calls=%async_computation.10 | async-start | bytes 10063872 | tf_op jit(solution)/shard_map/reduce_scatter | solution.py:67
  861.2 183.5 %copy-start.46 = (f32[512]{0:T(512)S(1)}, f32[512]{0:T(512)}, u32[]{:S(2)}) copy-start(f32[512]{0:T(512)} %copy-done.45) | copy-start | bytes 6148
  861.2 183.5 %copy-start.59 = (f32[512]{0:T(512)S(1)}, f32[512]{0:T(512)}, u32[]{:S(2)}) copy-start(f32[512]{0:T(512)} %param.25) | copy-start | bytes 6148
  861.2 185.6 %copy-start.55 = (f32[512]{0:T(512)S(1)}, f32[512]{0:T(512)}, u32[]{:S(2)}) copy-start(f32[512]{0:T(512)} %copy-done.54) | copy-start | bytes 6148
  861.2 185.6 %copy-start.51 = (f32[512]{0:T(512)S(1)}, f32[512]{0:T(512)}, u32[]{:S(2)}) copy-start(f32[512]{0:T(512)} %copy-done.50) | copy-start | bytes 6148
  861.2 185.6 %copy-start.66 = (f32[32]{0:T(128)S(1)}, f32[32]{0:T(128)}, u32[]{:S(2)}) copy-start(f32[32]{0:T(128)} %copy-done.65) | copy-start | bytes 388
  (66 other events, 466.5 us)
Sparse Core Ops, SparseCore 0:
  141.0 91.8 all-reduce.5
  638.1 86.5 all-reduce.7
  832.3 211.0 all-reduce.9
Sparse Core Ops, SparseCore 1:
  143.4 95.0 all-gather.4
  240.9 89.7 all-gather.2
  515.0 115.8 reduce-scatter.4
  667.7 115.8 reduce-scatter.6
  843.5 99.9 reduce-scatter.10
  1099.3 73.7 reduce-scatter.8
where the time goes:
time: 1200 us
  waiting for transfers between devices  498 us (42%)
  matrix products  471 us (39%)
  other arithmetic  111 us (9%)
  local copies, waits for them, and re-layouts  67.1 us (6%)
  starting transfers between devices  20.8 us (2%)
  between operations  16.7 us (1%)
    dot_general x38, matrix products, dot(): return jnp.einsum(eq, a, b, preferred_element_type=F32)  433 us
    psum x1, waiting for transfers between devices, shards(): lax.psum((routed_block.astype(F32) + shared_result).astype(BF), 'tensor')  179 us
    reduce_scatter x1, waiting for transfers between devices, shards(): lax.psum_scatter(mid_part.astype(BF), 'dp', scatter_dimension=0, tiled=True)  95.9 us
    psum x1, waiting for transfers between devices, shards(): lax.psum(jnp.dot(attended, w_out, preferred_element_type=F32).astype(BF),...  91.4 us
    all_gather x1, waiting for transfers between devices, shards(): hidden_all = lax.all_gather(hidden_mid, 'dp', tiled=True)  59.2 us
    psum x1, waiting for transfers between devices, shards(): lax.psum((mid_block.astype(F32) + mid_from_shared).astype(BF), 'tensor')  46.8 us
    concatenate x1, local copies, waits for them, and re-layouts, scatter_sum(): joined = jnp.concatenate(parts, axis=1)  40.1 us
    ppermute x8, waiting for transfers between devices, passed_along(): return lax.ppermute(shard, axis, pairs)  25.1 us
  transfers between devices with their start and end apart: 17, of which 7 were waited for; matrix products, arithmetic and copies ran while one was open for 29% of the time, Pallas kernels for 0%

commit v1 on v0

--- a/solution.py
+++ b/solution.py
@@ -1,7 +1,9 @@
+import functools
 import jax
 import jax.numpy as jnp
 from jax import lax
 from jax.sharding import PartitionSpec as P
+from jax.lax import axis_index, ppermute, psum
 
 DN = 128
 DR = 64
@@ -12,6 +14,36 @@
 BF = jnp.bfloat16
 F32 = jnp.float32
 epsilon = 1e-06
+
+
+def manage_the_slot(s0, dimension_no):
+    s0 = jnp.moveaxis(s0, 0, dimension_no)
+    low = s0.shape
+    return s0.reshape(
+        *low[:dimension_no], low[dimension_no] * low[dimension_no + 1], *low[dimension_no + 2 :]
+    )
+
+
+def take_loads_all(mine_x, axis_tag):
+    n_slots = psum(1, axis_tag)
+    odd = mine_x[None]
+    for pp in range(n_slots.bit_length() - 1):
+        all_rows = 1 << pp
+        views = []
+        for dd in range(n_slots):
+            views.append((dd, dd ^ all_rows))
+        moved = ppermute(odd, axis_tag, views)
+        base_arr = jnp.stack([odd, moved], axis=0)
+        side_arr = axis_index(axis_tag) >> pp & 1
+        odd = jnp.where(side_arr == 0, base_arr, base_arr[::-1]).reshape(-1, *mine_x.shape)
+    return odd
+
+
+def see_the_gates(target, q_in, pos_dim):
+    return manage_the_slot(take_loads_all(target, q_in), pos_dim)
+
+
+replace_shapes = functools.partial(see_the_gates, q_in="dp", pos_dim=0)
 
 
 def dot(eq, a, b):
@@ -149,7 +181,7 @@
     ).astype(F32)
     middle = token_features + attention
     hidden_mid = normed(middle, middle_gain).astype(BF)
-    hidden_all = lax.all_gather(hidden_mid, "dp", tiled=True)
+    hidden_all = replace_shapes(hidden_mid)
     shared_gate_val = jnp.dot(hidden_mid, shared_gate, preferred_element_type=F32)
     shared_up_val = jnp.dot(hidden_mid, shared_up, preferred_element_type=F32)
     shared_active = silu_gate(shared_gate_val, shared_up_val).astype(BF)

time: 1200 us -> 1480 us (1.23)
  blocking collectives: 9.42 us -> 185 us
  other arithmetic: 111 us -> 175 us
  waiting for transfers between devices: 498 us -> 531 us
    all_gather x1, blocking collectives: 9.42 us -> 185 us  [shards(): route_all = lax.all_gather(route_ids, 'dp', tiled=True)]
    ppermute x0 -> x3, waiting for transfers between devices: none -> 95.9 us  [take_loads_all(): moved = ppermute(odd, axis_tag, views)]
    all_gather x1 -> x0, waiting for transfers between devices: 59.2 us -> none  [shards(): hidden_all = lax.all_gather(hidden_mid, 'dp', tiled=True)]
    another operation x5 -> x9, other arithmetic: 3.56 us -> 32.6 us  [the longest x4 29 us: take_loads_all(): base_arr = jnp.stack([odd, moved], axis=0)]
    select_n x0 -> x2, other arithmetic: none -> 28.2 us  [take_loads_all(): jnp.where(side_arr == 0, base_arr, base_arr[::-1])]
  transfers between devices with their start and end apart: 17 -> 19, of which waited for: 7 -> 9; matrix products, arithmetic and copies ran while one was open for 29% -> 31% of each run, Pallas kernels for 0% -> 0%
where the time goes in v1:
time: 1480 us; the launch traced here: 1470 us
  waiting for transfers between devices  531 us (36%)
  matrix products  470 us (32%)
  blocking collectives  185 us (12%)
  other arithmetic  175 us (12%)
  local copies, waits for them, and re-layouts  68.6 us (5%)
  starting transfers between devices  24.1 us (2%)
  between operations  16.7 us (1%)
    dot_general x38, matrix products, dot(): return jnp.einsum(eq, a, b, preferred_element_type=F32)  435 us
    all_gather x1, blocking collectives, shards(): route_all = lax.all_gather(route_ids, 'dp', tiled=True)  185 us
    psum x1, waiting for transfers between devices, shards(): lax.psum((routed_block.astype(F32) + shared_result).astype(BF), 'tensor')  171 us
    ppermute x3, waiting for transfers between devices, take_loads_all(): moved = ppermute(odd, axis_tag, views)  95.9 us
    reduce_scatter x1, waiting for transfers between devices, shards(): lax.psum_scatter(mid_part.astype(BF), 'dp', scatter_dimension=0, tiled=True)  93.6 us
    psum x1, waiting for transfers between devices, shards(): lax.psum(jnp.dot(attended, w_out, preferred_element_type=F32).astype(BF),...  90.8 us
    psum x1, waiting for transfers between devices, shards(): lax.psum((mid_block.astype(F32) + mid_from_shared).astype(BF), 'tensor')  46.4 us
    concatenate x1, local copies, waits for them, and re-layouts, scatter_sum(): joined = jnp.concatenate(parts, axis=1)  40.2 us
  transfers between devices with their start and end apart: 19, of which 9 were waited for; matrix products, arithmetic and copies ran while one was open for 31% of the time, Pallas kernels for 0%

profile of v1, /device:TPU:0, one launch (start us, length us, event | category | flops | bytes accessed | tf_op | source)
XLA Modules:
  0.0 1469.8 jit_solution(14222011815443711639)
XLA Ops:
  40.0 25.1 %collective-permute-done = bf16[512,576]{0,1:T(8,128)(2,1)} collective-permute-done((bf16[512,576]{0,1:T(8,128)(2,1)}, bf16[512,576]{0,1:T(8,128)(2,1)}, u32[]{:S(2)}, u32[]{:S(2)}) %collective-permute-start) | collective-permute-done | bytes 589856 | tf_op jit(solution)/shard_map/ppermute | solution.py:56
  73.2 8.9 fusion.84
  82.2 13.6 fusion.3
  95.8 23.7 %fusion.171 = (f32[4,512]{1,0:T(4,128)S(1)}, f32[4,512,2560]{2,1,0:T(8,128)}) fusion(f32[4,512,2560]{2,1,0:T(8,128)} %fusion.3), kind=kOutput, calls=%fused_computation.259 | output fusion | flops 10488319 | bytes 41951232 | tf_op jit(solution)/shard_map/sub | solution.py:174
  119.5 17.4 %fusion.107 = bf16[4,128,512]{2,1,0:T(8,128)(2,1)} fusion(bf16[2560,4,256]{0,2,1:T(8,128)(2,1)} %bitcast.248, f32[4,512]{1,0:T(4,128)S(1)} %get-tuple-element.146, f32[4,512,2560]{2,1,0:T(8,128)} %fusion.3), kind=kOutput, calls=%fused_computation.155 | convolution fusion | flops 1358172672 | bytes 45096960 | tf_op jit(solution)/shard_map/hqk,khd->qhd/dot_general | solution.py:50
  142.4 90.8 %all-reduce.6.cloned.1.call-done = bf16[512,2048]{1,0:T(8,128)(2,1)} async-done(((bf16[512,2048]{1,0:T(8,128)(2,1)}), bf16[512,2048]{1,0:T(8,128)(2,1)}) %all-reduce.6.cloned.1.call-update) | async-done | bytes 2097168 | tf_op jit(solution)/shard_map/psum | solution.py:179
  252.9 91.4 %collective-permute-done.5 = bf16[2,512,2048]{2,1,0:T(8,128)(2,1)} collective-permute-done((bf16[2,512,2048]{2,1,0:T(8,128)(2,1)}, bf16[2,512,2048]{2,1,0:T(8,128)(2,1)}, u32[]{:S(2)}, u32[]{:S(2)}) %collective-permute-start.5) | collective-permute-done | bytes 4194336 | tf_op jit(solution)/shard_map/ppermute | solution.py:35
  352.0 14.2 reverse_select_fusion.1
  367.6 184.8 %all_gather.6 = s32[4096,6]{0,1:T(8,128)S(1)} all-gather(s32[512,6]{0,1:T(8,128)S(1)} %copy-done.62), channel_id=1, replica_groups=mesh['dp'=8,'tensor'=4] {'dp'}, dimensions={0}, use_global_device_ids=true | all-gather | bytes 110592 | tf_op jit(solution)/shard_map/all_gather | solution.py:136
  556.0 13.8 pad_maximum_fusion
  569.8 14.0 reverse_select_fusion
  591.2 18.8 %convolution_convert_fusion.1 = bf16[8,8,72,2048]{3,2,1,0:T(8,128)(2,1)} fusion(bf16[8,512,2048,1]{2,1,3,0:T(8,128)(2,1)} %bitcast.235, s32[8,8,512]{2,1,0:T(8,128)S(1)} %fusion.122), kind=kOutput, calls=%fused_computation.29 | convolution fusion | flops 9675472896 | bytes 35782656 | tf_op jit(solution)/shard_map/bect,btd->becd/dot_general | solution.py:50
  610.0 20.2 %fusion.18 = f32[8,8,72,352]{3,2,1,0:T(8,128)} fusion(bf16[8,8,72,2048]{3,2,1,0:T(8,128)(2,1)} %convolution_convert_fusion.1, bf16[8,2048,352]{1,2,0:T(8,128)(2,1)} %param.31), kind=kOutput, calls=%fused_computation.24 | convolution fusion | flops 6643777536 | bytes 36896768 | tf_op jit(solution)/shard_map/becd,edf->becf/dot_general | solution.py:50
  630.2 20.0 %fusion.20 = f32[8,8,72,352]{3,2,1,0:T(8,128)} fusion(bf16[8,8,72,2048]{3,2,1,0:T(8,128)(2,1)} %convolution_convert_fusion.1, bf16[8,2048,352]{1,2,0:T(8,128)(2,1)} %param.30), kind=kOutput, calls=%fused_computation.26 | convolution fusion | flops 6643777536 | bytes 36896768 | tf_op jit(solution)/shard_map/becd,edf->becf/dot_general | solution.py:50
  650.3 18.7 %convolution_convert_fusion = bf16[8,8,72,2048]{3,2,1,0:T(8,128)(2,1)} fusion(bf16[8,512,2048,1]{2,1,3,0:T(8,128)(2,1)} %bitcast.259, s32[8,8,512]{2,1,0:T(8,128)S(1)} %fusion.122), kind=kOutput, calls=%fused_computation.28 | convolution fusion | flops 9675472896 | bytes 35782656 | tf_op jit(solution)/shard_map/bect,btd->becd/dot_general | solution.py:50
  669.0 24.5 %fusion.39 = (bf16[8,8,72]{2,0,1:T(8,128)(2,1)S(1)}, bf16[8,8,72,352]{3,2,0,1:T(8,128)(2,1)}, f32[8,8,72,352]{3,2,1,0:T(8,128)}) fusion(f32[8,8,72,352]{3,2,1,0:T(8,128)} %fusion.18, f32[8,8,72,352]{3,2,1,0:T(8,128)} %fusion.20, bf16[8,352,2048]{2,1,0:T(8,128)(2,1)} %param.32, bf16[8,8,72,2048]{3,2,1,0:T(8,128)(2,1)} %convolution_convert_fusion), kind=kOutput, calls=%fused_computation.60 | convolution fusion | flops 6658371072 | bytes 53126144 | tf_op jit(solution)/shard_map/becd,efd->becf/dot_general | solution.py:50
  698.2 12.9 multiply_convert_fusion.1
  711.1 21.2 %fusion.31 = f32[8,8,72,2048]{3,2,0,1:T(8,128)} fusion(bf16[8,2048,352]{1,2,0:T(8,128)(2,1)} %param.30, bf16[8,8,72,352]{3,2,0,1:T(8,128)(2,1)} %get-tuple-element.115), kind=kOutput, calls=%fused_computation.36 | convolution fusion | flops 6643777536 | bytes 52527104 | tf_op jit(solution)/shard_map/becf,edf->becd/dot_general | solution.py:50
  732.3 40.2 %fusion.5 = f32[8,512,2048,1]{2,1,3,0:T(8,128)} fusion(f32[8,8,72,2048]{3,2,0,1:T(8,128)} %fusion.31, bf16[8,2048,352]{1,2,0:T(8,128)(2,1)} %param.31, bf16[8,8,72,352]{3,2,0,1:T(8,128)(2,1)} %get-tuple-element.114, pred[8,8,72,512]{3,2,1,0:T(8,128)(4,1)} %iota_compare_fusion.14), kind=kOutput, calls=%fused_computation.13 | convolution fusion | flops 16326328320 | bytes 88440832 | tf_op jit(solution)/shard_map/bect,becd->btd/dot_general | solution.py:50
  772.5 17.1 %fusion.1 = bf16[4096,2048]{1,0:T(8,128)(2,1)} fusion(f32[8,512,2048,1]{2,1,3,0:T(8,128)} %fusion.5, bf16[4096,64]{0,1:T(8,128)(2,1)} %multiply_convert_fusion.6, bf16[2048,64]{0,1:T(8,128)(2,1)S(1)} %copy-done.33), kind=kOutput, calls=%fused_computation.3 | convolution fusion | flops 1090519040 | bytes 51118080 | tf_op jit(solution)/shard_map/te,de->td/dot_general | solution.py:50
  810.5 93.6 %reduce-scatter.5.cloned.1.call-done = bf16[512,2048]{1,0:T(8,128)(2,1)} async-done(((bf16[4096,2048]{1,0:T(8,128)(2,1)}), bf16[512,2048]{1,0:T(8,128)(2,1)}) %reduce-scatter.5.cloned.1.call-update) | async-done | bytes 2097168 | tf_op jit(solution)/shard_map/reduce_scatter | solution.py:246
  911.7 29.4 %bitcast_convert_fusion = bf16[8,512,2048]{2,1,0:T(8,128)(2,1)} fusion(bf16[8,352,2048]{2,1,0:T(8,128)(2,1)} %param.32, bf16[8,8,72,352]{3,2,0,1:T(8,128)(2,1)} %get-tuple-element.138, pred[8,8,72,512]{3,2,1,0:T(8,128)(4,1)} %iota_compare_fusion.13), kind=kOutput, calls=%fused_computation.4 | convolution fusion | flops 16325279744 | bytes 33914880 | tf_op jit(solution)/shard_map/bect,becd->btd/dot_general | solution.py:50
  941.2 10.2 convolution_convert_fusion.11
  951.4 46.4 %all-reduce.8.cloned.1.call-done = bf16[512,2048]{1,0:T(8,128)(2,1)} async-done(((bf16[512,2048]{1,0:T(8,128)(2,1)}), bf16[512,2048]{1,0:T(8,128)(2,1)}) %all-reduce.8.cloned.1.call-update) | async-done | bytes 2097168 | tf_op jit(solution)/shard_map/psum | solution.py:247
  1008.3 19.6 %fusion.69 = bf16[2560,4,128]{0,2,1:T(8,128)(2,1)} fusion(bf16[512,4,128]{0,2,1:T(8,128)(2,1)} %bitcast.262, f32[4,512]{1,0:T(4,128)S(1)} %copy-done.50, f32[4,512,2560]{2,1,0:T(8,128)} %fusion.3), kind=kOutput, calls=%fused_computation.112 | convolution fusion | flops 1359221248 | bytes 24125440 | tf_op jit(solution)/shard_map/hqk,qhd->khd/dot_general | solution.py:50
  1028.0 15.2 %multiply_reduce_fusion = (f32[4,512]{1,0:T(4,128)S(1)}, f32[4,512,2560]{2,1,0:T(8,128)}) fusion(f32[4,512,2560]{2,1,0:T(8,128)} %get-tuple-element.147, f32[4,512]{1,0:T(4,128)S(1)} %copy-done.50, bf16[512,4,128]{0,2,1:T(8,128)(2,1)} %bitcast.263, bf16[2560,4,256]{0,2,1:T(8,128)(2,1)} %bitcast.249), kind=kOutput, calls=%fused_computation.10 | convolution fusion | flops 1357903872 | bytes 45105152 | tf_op jit(solution)/shard_map/qhd,khd->hqk/dot_general | solution.py:50
  1043.2 14.7 multiply_convert_fusion
  1146.5 171.4 %all-reduce.10.cloned.1.call-done = (bf16[512,2048]{1,0:T(8,128)(2,1)}, bf16[512,2048]{1,0:T(8,128)(2,1)}, bf16[512,576]{0,1:T(8,128)(2,1)}, bf16[2048,64]{0,1:T(8,128)(2,1)}) async-done(((bf16[512,2048]{1,0:T(8,128)(2,1)}, bf16[512,2048]{1,0:T(8,128)(2,1)}, bf16[512,576]{0,1:T(8,128)(2,1)}, bf16[2048,64]{0,1:T(8,128)(2,1)}), (bf16[512,2048]{1,0:T(8,128)(2,1)}, bf16[512,2048]{1,0:T(8,128)(2,1)}, ...) | async-done | bytes 5046288 | tf_op jit(solution)/shard_map/psum | solution.py:304
  1333.7 40.2 %concatenate.47 = bf16[2048,2179]{0,1:T(8,128)(2,1)} concatenate(bf16[2048,512]{0,1:T(8,128)(2,1)} %convolution_convert_fusion.8, bf16[2048,768]{0,1:T(8,128)(2,1)} %convolution_convert_fusion.3, bf16[2048,576]{0,1:T(8,128)(2,1)} %convolution_convert_fusion.7, bf16[2048,256]{0,1:T(8,128)(2,1)} %copy.126, bf16[2048,64]{0,1:T(8,128)(2,1)S(1)} %copy-done.41, ...), dimensions={1} | concatenate | bytes 17850368 | tf_op jit(solution)/shard_map/concatenate | solution.py:98
  1376.5 21.4 %convolution_bitcast_fusion = f32[8,2048,352]{1,2,0:T(8,128)} fusion(bf16[8,8,72,2048]{3,2,1,0:T(8,128)(2,1)} %convolution_convert_fusion.1, bf16[8,8,72,352]{3,2,0,1:T(8,128)(2,1)} %get-tuple-element.114), kind=kOutput, calls=%fused_computation.57 | convolution fusion | flops 6643777536 | bytes 45187072 | tf_op jit(solution)/shard_map/becd,becf->edf/dot_general | solution.py:50
  1397.9 22.3 %convolution_bitcast_fusion.1 = f32[8,2048,352]{1,2,0:T(8,128)} fusion(bf16[8,8,72,2048]{3,2,1,0:T(8,128)(2,1)} %convolution_convert_fusion.1, bf16[8,8,72,352]{3,2,0,1:T(8,128)(2,1)S(1)} %copy-done.9), kind=kOutput, calls=%fused_computation.58 | convolution fusion | flops 6643777536 | bytes 45187072 | tf_op jit(solution)/shard_map/becd,becf->edf/dot_general | solution.py:50
  1420.2 18.2 %fusion.35 = f32[8,352,2048]{2,1,0:T(8,128)} fusion(bf16[8,8,72,352]{3,2,0,1:T(8,128)(2,1)} %get-tuple-element.138, bf16[8,8,72,2048]{3,2,1,0:T(8,128)(2,1)} %convolution_convert_fusion), kind=kOutput, calls=%fused_computation.56 | convolution fusion | flops 6643777536 | bytes 45187072 | tf_op jit(solution)/shard_map/becf,becd->efd/dot_general | solution.py:50
  (297 shorter events, 259.0 us)
Async XLA Ops:
  8.0 225.2 %all-reduce.6.cloned.1.call-start = ((), (), s32[]{:S(2)}) async-start(), calls=%async_computation.4 | async-start | bytes 4194304 | tf_op jit(solution)/shard_map/psum | solution.py:179
  20.9 44.2 %collective-permute-start = (bf16[512,576]{0,1:T(8,128)(2,1)}, bf16[512,576]{0,1:T(8,128)(2,1)}, u32[]{:S(2)}, u32[]{:S(2)}) collective-permute-start(bf16[512,576]{0,1:T(8,128)(2,1)} %pad_maximum_fusion.7), channel_id=1, source_target_pairs={{0,16},{4,20},{8,24},{12,28},{1,17},{5,21},{9,25},{13,29},{2,18},{... | collective-permute-start | bytes 1769480 | tf_op jit(solution)/shard_map/ppermute | solution.py:56
  26.6 39.6 %collective-permute-start.1 = (bf16[512,576]{0,1:T(8,128)(2,1)}, bf16[512,576]{0,1:T(8,128)(2,1)}, u32[]{:S(2)}, u32[]{:S(2)}) collective-permute-start(bf16[512,576]{0,1:T(8,128)(2,1)} %pad_maximum_fusion.7), channel_id=1, source_target_pairs={{0,12},{4,16},{8,20},{12,24},{16,28},{1,13},{5,17},{9,21},{13,25},... | collective-permute-start | bytes 1769480 | tf_op jit(solution)/shard_map/ppermute | solution.py:56
  30.0 37.3 %collective-permute-start.2 = (bf16[512,576]{0,1:T(8,128)(2,1)}, bf16[512,576]{0,1:T(8,128)(2,1)}, u32[]{:S(2)}, u32[]{:S(2)}) collective-permute-start(bf16[512,576]{0,1:T(8,128)(2,1)} %pad_maximum_fusion.7), channel_id=1, source_target_pairs={{0,8},{4,12},{8,16},{12,20},{16,24},{20,28},{1,9},{5,13},{9,17},{1... | collective-permute-start | bytes 1769480 | tf_op jit(solution)/shard_map/ppermute | solution.py:56
  33.0 35.5 %collective-permute-start.3 = (bf16[512,576]{0,1:T(8,128)(2,1)}, bf16[512,576]{0,1:T(8,128)(2,1)}, u32[]{:S(2)}, u32[]{:S(2)}) collective-permute-start(bf16[512,576]{0,1:T(8,128)(2,1)} %pad_maximum_fusion.7), channel_id=1, source_target_pairs={{0,4},{4,8},{8,12},{12,16},{16,20},{20,24},{24,28},{1,5},{5,9},{9,... | collective-permute-start | bytes 1769480 | tf_op jit(solution)/shard_map/ppermute | solution.py:56
  39.9 33.3 %copy-start.24 = (f32[512,768]{0,1:T(8,128)}, f32[512,768]{0,1:T(8,128)S(1)}, u32[]{:S(2)}) copy-start(f32[512,768]{0,1:T(8,128)S(1)} %fusion.161) | copy-start | bytes 4718596
  40.0 42.2 %copy-start.28 = (bf16[512,4,32]{0,2,1:T(8,128)(2,1)}, bf16[512,4,32]{0,2,1:T(8,128)(2,1)S(1)}, u32[]{:S(2)}) copy-start(bf16[512,4,32]{0,2,1:T(8,128)(2,1)S(1)} %get-tuple-element.127) | copy-start | bytes 393220
  40.0 42.2 %copy-start.30 = (bf16[512,4,32]{0,2,1:T(8,128)(2,1)}, bf16[512,4,32]{0,2,1:T(8,128)(2,1)S(1)}, u32[]{:S(2)}) copy-start(bf16[512,4,32]{0,2,1:T(8,128)(2,1)S(1)} %get-tuple-element.128) | copy-start | bytes 393220
  141.2 95.7 %copy-start.43 = (f32[2048]{0:T(1024)S(1)}, f32[2048]{0:T(1024)}, u32[]{:S(2)}) copy-start(f32[2048]{0:T(1024)} %param.28) | copy-start | bytes 24580
  141.3 509.0 %all-gather.2.cloned.1.call-start = ((), (), s32[]{:S(2)}) async-start(), calls=%async_computation.5 | async-start | bytes 18874368 | tf_op jit(solution)/shard_map/all_gather | solution.py:135
  141.8 762.2 %reduce-scatter.5.cloned.1.call-start = ((), (), s32[]{:S(2)}) async-start(), calls=%async_computation.6 | async-start | bytes 18874368 | tf_op jit(solution)/shard_map/reduce_scatter | solution.py:246
  239.4 4.5 collective-permute-start.4
  251.4 92.9 %collective-permute-start.5 = (bf16[2,512,2048]{2,1,0:T(8,128)(2,1)}, bf16[2,512,2048]{2,1,0:T(8,128)(2,1)}, u32[]{:S(2)}, u32[]{:S(2)}) collective-permute-start(bf16[2,512,2048]{2,1,0:T(8,128)(2,1)} %get-tuple-element.119), channel_id=1, source_target_pairs={{0,8},{4,12},{8,0},{12,4},{16,24},{20,28},{24,16},{28,20},{1,9},{5... | collective-permute-start | bytes 12582920 | tf_op jit(solution)/shard_map/ppermute | solution.py:35
  366.2 189.9 %collective-permute-start.6 = (bf16[4,512,2048]{2,1,0:T(8,128)(2,1)}, bf16[4,512,2048]{2,1,0:T(8,128)(2,1)}, u32[]{:S(2)}, u32[]{:S(2)}) collective-permute-start(bf16[4,512,2048]{2,1,0:T(8,128)(2,1)} %bitcast.238), channel_id=1, source_target_pairs={{0,16},{4,20},{8,24},{12,28},{16,0},{20,4},{24,8},{28,12},{1,17},{... | collective-permute-start | bytes 25165832 | tf_op jit(solution)/shard_map/ppermute | solution.py:35
  732.3 40.2 %copy-start.33 = (bf16[2048,64]{0,1:T(8,128)(2,1)S(1)}, bf16[2048,64]{0,1:T(8,128)(2,1)}, u32[]{:S(2)}) copy-start(bf16[2048,64]{0,1:T(8,128)(2,1)} %param.29) | copy-start | bytes 786436
  789.6 208.2 %all-reduce.8.cloned.1.call-start = ((), (), s32[]{:S(2)}) async-start(), calls=%async_computation.8 | async-start | bytes 4194304 | tf_op jit(solution)/shard_map/psum | solution.py:247
  911.2 194.3 %reduce-scatter.7.cloned.1.call-start = ((), (), s32[]{:S(2)}) async-start(), calls=%async_computation.7 | async-start | bytes 18874368 | tf_op jit(solution)/shard_map/reduce_scatter | solution.py:250
  941.1 56.7 %copy-start.44 = (f32[2048]{0:T(1024)S(1)}, f32[2048]{0:T(1024)}, u32[]{:S(2)}) copy-start(f32[2048]{0:T(1024)} %param.28) | copy-start | bytes 24580
  941.1 56.7 %copy-start.46 = (f32[512]{0:T(512)S(1)}, f32[512]{0:T(512)}, u32[]{:S(2)}) copy-start(f32[512]{0:T(512)} %copy-done.45) | copy-start | bytes 6148
  941.1 376.7 %all-reduce.10.cloned.1.call-start = ((), (), s32[]{:S(2)}) async-start(), calls=%async_computation.11 | async-start | bytes 10092544 | tf_op jit(solution)/shard_map/psum | solution.py:304
  951.4 51.3 %copy-start.59 = (f32[512]{0:T(512)S(1)}, f32[512]{0:T(512)}, u32[]{:S(2)}) copy-start(f32[512]{0:T(512)} %copy-done.58) | copy-start | bytes 6148
  1075.7 21.0 %collective-permute-start.10 = (bf16[512,576]{0,1:T(8,128)(2,1)}, bf16[512,576]{0,1:T(8,128)(2,1)S(1)}, u32[]{:S(2)}, u32[]{:S(2)}) collective-permute-start(bf16[512,576]{0,1:T(8,128)(2,1)} %get-tuple-element.121), channel_id=1, source_target_pairs={{4,0},{8,4},{12,8},{16,12},{20,16},{24,20},{28,24},{5,1},{9,5},{13... | collective-permute-start | bytes 1769480 | tf_op jit(solution)/shard_map/ppermute | solution.py:56
  1077.0 19.7 %collective-permute-start.7 = (bf16[512,576]{0,1:T(8,128)(2,1)}, bf16[512,576]{0,1:T(8,128)(2,1)S(1)}, u32[]{:S(2)}, u32[]{:S(2)}) collective-permute-start(bf16[512,576]{0,1:T(8,128)(2,1)} %get-tuple-element.120), channel_id=1, source_target_pairs={{16,0},{20,4},{24,8},{28,12},{17,1},{21,5},{25,9},{29,13},{18,2},{... | collective-permute-start | bytes 1769480 | tf_op jit(solution)/shard_map/ppermute | solution.py:56
  1078.3 18.4 %collective-permute-start.8 = (bf16[512,576]{0,1:T(8,128)(2,1)}, bf16[512,576]{0,1:T(8,128)(2,1)}, u32[]{:S(2)}, u32[]{:S(2)}) collective-permute-start(bf16[512,576]{0,1:T(8,128)(2,1)} %get-tuple-element.123), channel_id=1, source_target_pairs={{12,0},{16,4},{20,8},{24,12},{28,16},{13,1},{17,5},{21,9},{25,13},... | collective-permute-start | bytes 1769480 | tf_op jit(solution)/shard_map/ppermute | solution.py:56
  1079.6 23.4 %collective-permute-start.9 = (bf16[512,576]{0,1:T(8,128)(2,1)S(1)}, bf16[512,576]{0,1:T(8,128)(2,1)}, u32[]{:S(2)}, u32[]{:S(2)}) collective-permute-start(bf16[512,576]{0,1:T(8,128)(2,1)S(1)} %get-tuple-element.122), channel_id=1, source_target_pairs={{8,0},{12,4},{16,8},{20,12},{24,16},{28,20},{9,1},{13,5},{17,9},{2... | collective-permute-start | bytes 1769480 | tf_op jit(solution)/shard_map/ppermute | solution.py:56
  1111.4 262.5 %reduce-scatter.11.cloned.1.call-start = ((), (), s32[]{:S(2)}) async-start(), calls=%async_computation.10 | async-start | bytes 9732096 | tf_op jit(solution)/shard_map/reduce_scatter | solution.py:99
  1124.2 323.5 %reduce-scatter.9.cloned.1.call-start = ((), (), s32[]{:S(2)}) async-start(), calls=%async_computation.9 | async-start | bytes 10063872 | tf_op jit(solution)/shard_map/reduce_scatter | solution.py:99
  1143.0 176.3 %copy-start.48 = (f32[512]{0:T(512)S(1)}, f32[512]{0:T(512)}, u32[]{:S(2)}) copy-start(f32[512]{0:T(512)} %copy-done.47) | copy-start | bytes 6148
  1143.0 176.3 %copy-start.61 = (f32[512]{0:T(512)S(1)}, f32[512]{0:T(512)}, u32[]{:S(2)}) copy-start(f32[512]{0:T(512)} %param.25) | copy-start | bytes 6148
  1143.0 178.3 %copy-start.57 = (f32[512]{0:T(512)S(1)}, f32[512]{0:T(512)}, u32[]{:S(2)}) copy-start(f32[512]{0:T(512)} %copy-done.56) | copy-start | bytes 6148
  1143.0 178.4 %copy-start.53 = (f32[512]{0:T(512)S(1)}, f32[512]{0:T(512)}, u32[]{:S(2)}) copy-start(f32[512]{0:T(512)} %copy-done.52) | copy-start | bytes 6148
  1143.0 178.4 %copy-start.68 = (f32[32]{0:T(128)S(1)}, f32[32]{0:T(128)}, u32[]{:S(2)}) copy-start(f32[32]{0:T(128)} %copy-done.67) | copy-start | bytes 388
  (64 other events, 491.8 us)
Sparse Core Ops, SparseCore 0:
  141.4 91.8 all-reduce.5
  911.4 86.4 all-reduce.7
  1111.5 206.2 all-reduce.9
Sparse Core Ops, SparseCore 1:
  143.8 95.0 all-gather.1
  789.7 114.3 reduce-scatter.4
  941.2 115.7 reduce-scatter.6
  1124.3 95.1 reduce-scatter.10
  1373.9 73.7 reduce-scatter.8
